TPU v7x, 32 devices: a whole 2x2x4 slice. The times are simulated.
32 devices in a mesh: row: 4 (over x, core), col: 8 (over z, y).
Axes of the slice: x: 2, y: 2, z: 4, core: 2. Of those that a mesh axis runs over, the one named last changes fastest.
Arguments:
- front_panels: float32 [16, 4, 256, 8, 8, 256], P(None, 'row', 'col'), as said below
- child_update_tiles: float32 [4, 8, 8, 256, 256], P('row', 'col'), may hold values from -2 to 2
- child_rows: int32 [4, 8, 8], P('row', 'col'), may hold values from 0 to 63, as said below
- child_cols: int32 [4, 8, 8], P('row', 'col'), may hold values from 0 to 7
- child_counts: int32 [4, 8], P('row', 'col'), may hold values from 4 to 8, as said below
- row_maps: int32 [4, 8, 8, 256], P('row', 'col'), may hold values from 0 to 255, each once within a row
- col_maps: int32 [4, 8, 8, 256], P('row', 'col'), may hold values from 0 to 255, each once within a row
Outputs:
- factored_front: float32 [16, 4, 256, 8, 8, 256], P(None, 'row', None, None, 'col')
Inputs may be any that keep to these rules, and one draw needn't show every extreme that they name: child_rows[r, c, k] modulo 4 names one of four owner rows; among the live slots of one device at most 2 name the same owner row, and some device sends exactly 2 to some owner; every slot's target tile column is at most its target tile row. `child_counts`: every device of col index 0 has all slots live. `front_panels`: the diagonal of the front dominates its first tile, so that tile stays positive definite after the children are added.
All inputs are finite; a program needn't handle non-finite values.
Results may differ from a plain program's by a relative error of at most 0.0003.
Values sent between devices are 32-bit elements; how exact they have to be, the bound alone decides.
No kernel may reach another device: no remote copies, remote signals or barrier semaphores. Data moves between devices by JAX's collectives and lax.ppermute only.
A program may use at most 320 MiB of HBM per device.

v0:
```python
import jax
import jax.numpy as jnp
from jax import lax
from jax.sharding import PartitionSpec as P


def broadcast(value, axis, source):
    kept = jnp.where(lax.axis_index(axis) == source, value, 0).astype(value.dtype)
    return lax.psum(kept, axis)


def slot_positions(owners, is_live):
    slot_entries = owners.shape[-1]
    earlier = lax.broadcasted_iota(
        jnp.int32, (slot_entries, slot_entries), 0
    ) < lax.broadcasted_iota(jnp.int32, (slot_entries, slot_entries), 1)
    same_owner = (owners[..., :, None] == owners[..., None, :]) & is_live[..., :, None] & earlier
    return jnp.sum(same_owner.astype(jnp.int32), axis=-2)


def on_device(
    front_panels, child_update_tiles, child_rows, child_cols, child_counts, row_maps, col_maps
):
    largest_index = lax.Precision.HIGHEST
    row_size = lax.axis_size("row")
    col_size = lax.axis_size("col")
    my_row = lax.axis_index("row")
    my_col = lax.axis_index("col")
    front_width = front_panels.shape[-1]
    blocks = lax.all_to_all(front_panels, "col", split_axis=4, concat_axis=2, tiled=True)
    row_tiles = blocks.shape[0]
    col_tiles = blocks.shape[3]
    blocks = blocks.reshape(row_tiles, front_width, col_tiles, front_width)
    slot_entries = child_update_tiles.shape[2]
    capacity = slot_entries // 4
    labels = lax.broadcasted_iota(jnp.int32, (1, 1, front_width), 2)
    row_indicator = (row_maps.reshape(slot_entries, front_width)[:, :, None] == labels).astype(
        jnp.float32
    )
    column_indicator = (col_maps.reshape(slot_entries, front_width)[:, :, None] == labels).astype(
        jnp.float32
    )
    shifted_tiles = jnp.einsum(
        "gml,gmq->glq",
        row_indicator,
        child_update_tiles.reshape(slot_entries, front_width, front_width),
        precision=largest_index,
    )
    shifted_tiles = jnp.einsum(
        "afb,abx->afx", shifted_tiles, column_indicator, precision=largest_index
    )
    slot_ids = lax.broadcasted_iota(jnp.int32, (slot_entries,), 0)
    is_live = slot_ids < child_counts.reshape(())
    owners = child_rows.reshape(slot_entries) % row_size
    positions = slot_positions(owners, is_live)
    dest_ids = lax.broadcasted_iota(jnp.int32, (row_size, capacity, slot_entries), 0)
    place_ids = lax.broadcasted_iota(jnp.int32, (row_size, capacity, slot_entries), 1)
    selector = (
        (owners[None, None, :] == dest_ids)
        & (positions[None, None, :] == place_ids)
        & is_live[None, None, :]
    ).astype(jnp.float32)
    outgoing = jnp.einsum(
        "opk,kx->opx",
        selector,
        shifted_tiles.reshape(slot_entries, front_width * front_width),
        precision=largest_index,
    )
    incoming = lax.all_to_all(outgoing, "row", split_axis=0, concat_axis=0, tiled=True)
    all_rows, all_cols, all_counts = (
        lax.all_gather(child_rows, "row", axis=0, tiled=True),
        lax.all_gather(child_cols, "row", axis=0, tiled=True),
        lax.all_gather(child_counts, "row", axis=0, tiled=True),
    )
    source_rows = all_rows.reshape(row_size, slot_entries)
    source_cols = all_cols.reshape(row_size, slot_entries)
    source_live = slot_ids[None, :] < all_counts.reshape(row_size)[:, None]
    source_owner = source_rows % row_size
    source_pos = slot_positions(source_owner, source_live)
    mine = (source_live & (source_owner == my_row)).astype(jnp.float32)
    depth_onehot = (
        (source_rows // row_size)[:, :, None]
        == lax.broadcasted_iota(jnp.int32, (1, 1, row_tiles), 2)
    ).astype(jnp.float32) * mine[:, :, None]
    across_onehot = (
        source_cols[:, :, None] == lax.broadcasted_iota(jnp.int32, (1, 1, col_tiles), 2)
    ).astype(jnp.float32)
    place_onehot = (
        source_pos[:, :, None] == lax.broadcasted_iota(jnp.int32, (1, 1, capacity), 2)
    ).astype(jnp.float32)
    landing = jnp.einsum(
        "ska,skb,skp->absp", depth_onehot, across_onehot, place_onehot, precision=largest_index
    )
    incoming = incoming.reshape(row_size, capacity, front_width, front_width)
    blocks = blocks + jnp.einsum("absp,spxy->axby", landing, incoming, precision=largest_index)
    tile_i = lax.broadcasted_iota(jnp.int32, (row_tiles, 1, col_tiles, 1), 0) * row_size + my_row
    tile_j = lax.broadcasted_iota(jnp.int32, (row_tiles, 1, col_tiles, 1), 2) * col_size + my_col
    flipped = jnp.einsum("axby->aybx", blocks)
    blocks = jnp.where(tile_i == tile_j, 0.5 * (blocks + flipped), blocks)
    identity = jnp.eye(front_width, dtype=jnp.float32)
    corner = blocks[0, :, 0, :]
    at_root = (my_row == 0) & (my_col == 0)
    factor = jnp.linalg.cholesky(jnp.where(at_root, corner, identity))
    factor = broadcast(factor, "row", 0)
    column = blocks[:, :, 0, :].reshape(row_tiles * front_width, front_width)
    solved = jax.scipy.linalg.solve_triangular(factor, column.T, lower=True).T.reshape(
        row_tiles, front_width, front_width
    )
    tile_index = lax.broadcasted_iota(jnp.int32, (row_tiles, 1, 1), 0) * row_size + my_row
    kept = jnp.where(tile_index == 0, factor[None, :, :], solved)
    below = jnp.where(tile_index == 0, 0.0, solved)
    row_panel = broadcast(below, "col", 0)
    group = col_size // row_size
    whole = lax.all_gather(row_panel, "row", axis=0, tiled=True)
    whole = whole.reshape(row_size, col_tiles, group, front_width, front_width)
    picked = lax.dynamic_index_in_dim(whole, my_col % row_size, 0, keepdims=False)
    col_panel = lax.dynamic_index_in_dim(picked, my_col // row_size, 1, keepdims=False)
    blocks = blocks - jnp.einsum("asx,bqx->asbq", row_panel, col_panel, precision=largest_index)
    first_column = jnp.where(my_col == 0, kept, blocks[:, :, 0, :])
    blocks = blocks.at[:, :, 0, :].set(first_column)
    blocks = jnp.where(tile_i >= tile_j, blocks, 0.0)
    return blocks.reshape(row_tiles, 1, front_width, col_tiles, 1, front_width)


def solution(mesh):
    return jax.shard_map(
        on_device,
        mesh=mesh,
        in_specs=(
            P(None, "row", "col", None, None, None),
            P("row", "col", None, None, None),
            P("row", "col", None),
            P("row", "col", None),
            P("row", "col"),
            P("row", "col", None, None),
            P("row", "col", None, None),
        ),
        out_specs=P(None, "row", None, None, "col", None),
        check_vma=False,
    )
```

profile of v0, /device:TPU:0, one launch (start us, length us, event | category | flops | bytes accessed | tf_op | source)
XLA Modules:
  0.0 1470.2 jit_solution(9605571834959242759)
XLA Ops:
  6.5 0.8 and_select_fusion.1
  8.1 2.2 fusion.8
  10.3 2.6 fusion.11
  13.0 2.0 reshape.354
  15.7 4.1 fusion.33
  19.8 4.2 all-to-all-start.1
  24.0 30.6 %copy.67 = f32[16,1,32,8,8,256]{5,3,2,0,1,4:T(8,128)} copy(f32[16,1,32,8,8,256]{5,4,3,2,1,0:T(8,128)} %param.9) | data formatting | bytes 67108864 | tf_op args[0]
  54.6 1.3 copy-done.4
  55.9 7.1 all-to-all-start
  64.2 5.8 all-reduce.1
  70.0 5.0 all_gather.14
  75.0 5.2 all_gather.17
  81.3 3.5 reshape.323
  84.8 30.9 %convolution_bitcast_fusion = f32[256,256,16,8]{1,2,3,0:T(8,128)} fusion(f32[4,2,256,256,1]{3,2,1,0,4:T(8,128)S(1)} %bitcast.110, f32[16,8,4,2]{0,1,3,2:T(8,128)S(1)} %convolution_bitcast_fusion.1), kind=kOutput, calls=%fused_computation.8 | convolution fusion | flops 805306368 | bytes 35655680 | tf_op jit(solution)/shard_map/absp,spxy->axby/dot_general | solution.py:95
  115.7 34.4 %copy.72 = f32[256,256,16,8]{0,1,3,2:T(8,128)} copy(f32[256,256,16,8]{1,2,3,0:T(8,128)} %convolution_bitcast_fusion) | data formatting | bytes 67108864 | tf_op jit(solution)/shard_map/absp,spxy->axby/dot_general | solution.py:95
  150.2 637.7 %all-to-all-done = f32[16,1,32,8,8,256]{5,3,2,0,1,4:T(8,128)} async-done(((f32[16,1,32,8,8,256]{5,3,2,0,1,4:T(8,128)}), f32[16,1,32,8,8,256]{5,3,2,0,1,4:T(8,128)}, u32[]{:S(2)}, u32[]{:S(2)}) %all-to-all-start) | async-done | bytes 33554464 | tf_op jit(solution)/shard_map/all_to_all | solution.py:30
  787.9 22.9 %copy.68 = f32[16,1,32,8,8,256]{5,3,2,4,0,1:T(8,128)} copy(f32[16,1,32,8,8,256]{5,3,2,0,1,4:T(8,128)} %all-to-all-done) | data formatting | bytes 67108864 | tf_op jit(solution)/shard_map/all_to_all | solution.py:30
  810.7 35.0 %copy.73 = f32[16,256,8,256]{1,3,2,0:T(8,128)} copy(f32[16,256,8,256]{3,2,1,0:T(8,128)} %bitcast.104) | data formatting | bytes 67108864 | tf_op jit(solution)/shard_map/reshape | solution.py:33
  845.7 33.5 %bitcast_add_fusion.1 = f32[16,256,8,256]{1,3,2,0:T(8,128)} fusion(f32[16,256,8,256]{1,3,2,0:T(8,128)} %copy.73, f32[256,256,16,8]{0,1,3,2:T(8,128)} %copy.72), kind=kLoop, calls=%fused_computation.5 | loop fusion | flops 8388608 | bytes 100663296 | tf_op jit(solution)/shard_map/add | solution.py:95
  879.2 31.9 %copy.74 = f32[16,256,8,256]{3,1,2,0:T(8,128)} copy(f32[16,256,8,256]{1,3,2,0:T(8,128)} %bitcast_add_fusion.1) | data formatting | bytes 67108864 | tf_op jit(solution)/shard_map/add | solution.py:95
  911.2 33.6 %fusion.1 = f32[16,256,8,256]{1,3,2,0:T(8,128)} fusion(f32[16,256,8,256]{1,3,2,0:T(8,128)} %bitcast_add_fusion.1, f32[16,256,8,256]{3,1,2,0:T(8,128)} %copy.74, pred[16,8]{1,0:T(8,128)(4,1)S(1)} %get-tuple-element.42), kind=kLoop, calls=%fused_computation.4 | loop fusion | flops 25165824 | bytes 100663424 | tf_op jit(solution)/shard_map/jit(_where)/select_n | solution.py:99
  944.8 1.0 fusion.14
  945.9 1.0 fusion.15
  947.0 11.7 cholesky.50
  958.7 9.8 custom-call.15
  969.0 11.7 cholesky.105
  983.6 4.5 slice.96
  988.1 5.8 copy.76
  993.9 5.7 copy.77
  999.6 14.6 all-reduce.5.cloned.1.call-done
  1014.1 1.0 fusion.16
  1015.2 3.9 while.2
  1015.8 1.3 bitcast_dynamic-update-slice_fusion.3
  1017.7 1.3 bitcast_dynamic-update-slice_fusion.3
  1019.0 19.7 %custom-call.16 = f32[2,128,128]{1,2,0:T(8,128)S(1)} custom-call(f32[2,128,128]{2,1,0:T(8,128)S(1)} %get-tuple-element.24), custom_call_target="InvertDiagBlocksLowerTriangular" | custom-call | tf_op jit(solution)/shard_map/jit(_solve_triangular)/triangular_solve | solution.py:106
  1038.7 3.6 fusion.4
  1042.4 1.9 convolution_subtract_fusion.1
  1044.3 1.9 fusion.18
  1046.3 2.4 maximum_bitcast_fusion
  1048.6 5.6 copy.94
  1054.2 4.7 select_select_fusion
  1059.0 156.4 %all-reduce.7.cloned.1.call-done = f32[16,256,256]{2,1,0:T(8,128)} async-done(((f32[16,256,256]{2,1,0:T(8,128)}), f32[16,256,256]{2,1,0:T(8,128)}) %all-reduce.7.cloned.1.call-update) | async-done | bytes 4194320 | tf_op jit(solution)/shard_map/psum | solution.py:9
  1215.5 5.6 copy.83
  1221.2 100.9 %all-gather.2.cloned.1.call-done = f32[64,256,256]{2,1,0:T(8,128)} async-done(((f32[16,256,256]{2,1,0:T(8,128)}), f32[64,256,256]{2,1,0:T(8,128)}) %all-gather.2.cloned.1.call-update) | async-done | bytes 16777232 | tf_op jit(solution)/shard_map/all_gather | solution.py:114
  1322.0 35.3 %convolution_subtract_fusion = f32[16,256,8,256]{1,3,2,0:T(8,128)} fusion(f32[16,256,8,256]{1,3,2,0:T(8,128)} %fusion.1, f32[16,256,256]{2,1,0:T(8,128)} %all-reduce.7.cloned.1.call-done, f32[4,8,2,256,256]{4,3,2,1,0:T(8,128)} %bitcast.111, s32[]{:T(128)S(6)} %select_n.139, s32[]{:T(128)S(6)} %select_n.142), kind=kOutput, calls=%fused_computation.7 | convolution fusion | flops 25778192384 | bytes 73400328 | tf_op jit(solution)/shard_map/asx,bqx->asbq/dot_general | solution.py:118
  1357.3 4.8 fusion.2
  1362.2 22.9 %select_bitcast_fusion = f32[16,1,256,8,1,256]{2,5,3,0,4,1:T(8,128)} fusion(f32[16,256,8,256]{1,3,2,0:T(8,128)} %fusion.2, pred[16,8]{1,0:T(8,128)(4,1)S(1)} %copy-done.6), kind=kLoop, calls=%fused_computation.6 | loop fusion | flops 8388608 | bytes 67108992 | tf_op jit(solution)/shard_map/reshape | solution.py:122
  1385.1 78.3 %copy.84 = f32[16,1,256,8,1,256]{5,4,3,2,1,0:T(1,128)} copy(f32[16,1,256,8,1,256]{2,5,3,0,4,1:T(8,128)} %select_bitcast_fusion) | data formatting | bytes 67108864 | tf_op jit(solution)/shard_map/reshape | solution.py:122
  (64 shorter events, 6.9 us)
Async XLA Ops:
  6.5 1.6 copy-start
  6.5 3.8 copy-start.7
  19.8 34.8 %all-to-all-start.1 = ((f32[4,2,65536]{2,1,0:T(2,128)}), f32[4,2,65536]{2,1,0:T(2,128)S(1)}, u32[]{:S(2)}, u32[]{:S(2)}) async-start(f32[4,2,65536]{2,1,0:T(2,128)} %fusion.33), calls=%async_computation.1 | async-start | bytes 4194304 | tf_op jit(solution)/shard_map/all_to_all | solution.py:69
  54.6 8.5 copy-start.10
  54.6 15.4 %copy-start.8 = (s32[1,1,8]{2,1,0:T(1,128)S(1)}, s32[1,1,8]{2,1,0:T(1,128)}, u32[]{:S(2)}) copy-start(s32[1,1,8]{2,1,0:T(1,128)} %param.11) | copy-start | bytes 100
  54.6 20.5 %copy-start.9 = (s32[1,1,8]{2,1,0:T(1,128)S(1)}, s32[1,1,8]{2,1,0:T(1,128)}, u32[]{:S(2)}) copy-start(s32[1,1,8]{2,1,0:T(1,128)} %param.12) | copy-start | bytes 100
  54.6 1.3 copy-start.4
  55.9 731.9 %all-to-all-start = ((f32[16,1,32,8,8,256]{5,3,2,0,1,4:T(8,128)}), f32[16,1,32,8,8,256]{5,3,2,0,1,4:T(8,128)}, u32[]{:S(2)}, u32[]{:S(2)}) async-start(f32[16,1,32,8,8,256]{5,3,2,0,1,4:T(8,128)} %copy.67), calls=%async_computation | async-start | bytes 67108864 | tf_op jit(solution)/shard_map/all_to_all | solution.py:30
  63.0 951.1 %all-reduce.5.cloned.1.call-start = ((), (), s32[]{:S(2)}) async-start(), calls=%async_computation.2 | async-start | bytes 524288 | tf_op jit(solution)/shard_map/psum | solution.py:9
  983.5 231.9 %all-reduce.7.cloned.1.call-start = ((), (), s32[]{:S(2)}) async-start(), calls=%async_computation.3 | async-start | bytes 8388608 | tf_op jit(solution)/shard_map/psum | solution.py:9
  1038.7 3.7 copy-start.3
  1059.0 263.1 %all-gather.2.cloned.1.call-start = ((), (), s32[]{:S(2)}) async-start(), calls=%async_computation.4 | async-start | bytes 20971520 | tf_op jit(solution)/shard_map/all_gather | solution.py:114
  1215.5 5.6 copy-start.5
  1322.0 35.3 %copy-start.2 = (f32[16,256,1,256]{1,3,2,0:T(8,128)S(1)}, f32[16,256,1,256]{1,3,2,0:T(8,128)}, u32[]{:S(2)}) copy-start(f32[16,256,1,256]{1,3,2,0:T(8,128)} %copy.83) | copy-start | bytes 12582916
  1357.3 4.8 copy-start.6
  1385.1 78.3 %copy-start.1 = (f32[1,1,8,256,256]{4,3,2,1,0:T(8,128)S(1)}, f32[1,1,8,256,256]{4,3,2,1,0:T(8,128)}, u32[]{:S(2)}) copy-start(f32[1,1,8,256,256]{4,3,2,1,0:T(8,128)} %param.10) | copy-start | bytes 6291460
Sparse Core Ops, SparseCore 0:
  983.6 30.4 all-reduce.4
  1059.1 156.2 all-reduce.6
  1217.1 104.9 all-gather.1
where the time goes:
time: 1480 us; the launch traced here: 1470 us
  waiting for transfers between devices  910 us (61%)
  local copies, waits for them, and re-layouts  273 us (18%)
  other arithmetic  162 us (11%)
  matrix products  83.3 us (6%)
  blocking collectives  16 us (1%)
  between operations  15.5 us (1%)
    all_to_all x1, waiting for transfers between devices, on_device(): lax.all_to_all(front_panels, 'col', split_axis=4, concat_axis=2, tiled=True)  638 us
    psum x2, waiting for transfers between devices, broadcast(): return lax.psum(kept, axis)  171 us
    all_gather x1, waiting for transfers between devices, on_device(): whole = lax.all_gather(row_panel, 'row', axis=0, tiled=True)  101 us
    reshape x1, local copies, waits for them, and re-layouts, on_device(): return blocks.reshape(row_tiles, 1, front_width, col_tiles, 1, front_width)  78.3 us
    dot_general x1, matrix products, on_device(): jnp.einsum('asx,bqx->asbq', row_panel, col_panel, precision=largest_index)  35.3 us
    reshape x1, local copies, waits for them, and re-layouts, on_device(): blocks = blocks.reshape(row_tiles, front_width, col_tiles, front_width)  35 us
    dot_general x1, local copies, waits for them, and re-layouts, on_device(): jnp.einsum('absp,spxy->axby', landing, incoming, precision=largest_index)  34.4 us
    another operation x6, other arithmetic, on_device(): factor = jnp.linalg.cholesky(jnp.where(at_root, corner, identity))  34 us
  transfers between devices with their start and end apart: 5, of which 4 were waited for; matrix products, arithmetic and copies ran while one was open for 8% of the time, Pallas kernels for 0%

commit v1 on v0

--- a/solution.py
+++ b/solution.py
@@ -2,6 +2,12 @@
 import jax.numpy as jnp
 from jax import lax
 from jax.sharding import PartitionSpec as P
+
+
+def joined_along(blocks, dim):
+    blocks = jnp.moveaxis(blocks, 0, dim)
+    lengths = blocks.shape
+    return blocks.reshape(*lengths[:dim], lengths[dim] * lengths[dim + 1], *lengths[dim + 2 :])
 
 
 def broadcast(value, axis, source):
@@ -111,7 +117,19 @@
     below = jnp.where(tile_index == 0, 0.0, solved)
     row_panel = broadcast(below, "col", 0)
     group = col_size // row_size
-    whole = lax.all_gather(row_panel, "row", axis=0, tiled=True)
+    size = lax.axis_size("row")
+    pairs = [(i, (i + 1) % size) for i in range(size)]
+    back = [(b, a) for a, b in pairs]
+    lower, upper = ([], [])
+    for step in range(size - 1):
+        if step % 2 == 0:
+            lower.append(lax.ppermute(lower[-1] if lower else row_panel, "row", pairs))
+        else:
+            upper.append(lax.ppermute(upper[-1] if upper else row_panel, "row", back))
+    pieces = jnp.stack([*lower[::-1], row_panel, *upper])
+    shift = lax.axis_index("row") - len(lower)
+    pieces = pieces[(jnp.arange(size) - shift) % size]
+    whole = joined_along(pieces, 0)
     whole = whole.reshape(row_size, col_tiles, group, front_width, front_width)
     picked = lax.dynamic_index_in_dim(whole, my_col % row_size, 0, keepdims=False)
     col_panel = lax.dynamic_index_in_dim(picked, my_col // row_size, 1, keepdims=False)

time: 1480 us -> 1550 us (1.047)
  waiting for transfers between devices: 910 us -> 941 us
  local copies, waits for them, and re-layouts: 273 us -> 294 us
  other arithmetic: 162 us -> 180 us
    ppermute x0 -> x3, waiting for transfers between devices: none -> 132 us  [the longest x2 132 us: on_device(): lower.append(lax.ppermute(lower[-1] if lower else row_panel, 'row', pairs))]
    all_gather x1 -> x0, waiting for transfers between devices: 101 us -> none  [on_device(): whole = lax.all_gather(row_panel, 'row', axis=0, tiled=True)]
    gather x0 -> x3, local copies, waits for them, and re-layouts: none -> 21.6 us  [on_device(): pieces = pieces[(jnp.arange(size) - shift) % size]]
    unnamed x26 -> x28, local copies, waits for them, and re-layouts: 33.2 us -> 33.4 us
  transfers between devices with their start and end apart: 5 -> 7, of which waited for: 4 -> 5; matrix products, arithmetic and copies ran while one was open for 8% -> 8% of each run, Pallas kernels for 0% -> 0%
where the time goes in v1:
time: 1550 us; the launch traced here: 1540 us
  waiting for transfers between devices  941 us (61%)
  local copies, waits for them, and re-layouts  294 us (19%)
  other arithmetic  180 us (12%)
  matrix products  82.8 us (5%)
  blocking collectives  16 us (1%)
  between operations  15.9 us (1%)
    all_to_all x1, waiting for transfers between devices, on_device(): lax.all_to_all(front_panels, 'col', split_axis=4, concat_axis=2, tiled=True)  638 us
    psum x2, waiting for transfers between devices, broadcast(): return lax.psum(kept, axis)  171 us
    ppermute x2, waiting for transfers between devices, on_device(): lower.append(lax.ppermute(lower[-1] if lower else row_panel, 'row', pairs))  132 us
    reshape x1, local copies, waits for them, and re-layouts, on_device(): return blocks.reshape(row_tiles, 1, front_width, col_tiles, 1, front_width)  78.3 us
    reshape x1, local copies, waits for them, and re-layouts, on_device(): blocks = blocks.reshape(row_tiles, front_width, col_tiles, front_width)  35 us
    dot_general x1, matrix products, on_device(): jnp.einsum('asx,bqx->asbq', row_panel, col_panel, precision=largest_index)  34.9 us
    dot_general x1, local copies, waits for them, and re-layouts, on_device(): jnp.einsum('absp,spxy->axby', landing, incoming, precision=largest_index)  34.4 us
    another operation x6, other arithmetic, on_device(): factor = jnp.linalg.cholesky(jnp.where(at_root, corner, identity))  34 us
  transfers between devices with their start and end apart: 7, of which 5 were waited for; matrix products, arithmetic and copies ran while one was open for 8% of the time, Pallas kernels for 0%

profile of v1, /device:TPU:0, one launch (start us, length us, event | category | flops | bytes accessed | tf_op | source)
XLA Modules:
  0.0 1543.1 jit_solution(7049445988811103189)
XLA Ops:
  8.1 2.2 fusion.8
  10.3 2.6 fusion.11
  13.0 2.0 reshape.415
  15.7 4.1 fusion.33
  19.8 4.2 all-to-all-start.1
  24.0 30.6 %copy.67 = f32[16,1,32,8,8,256]{5,3,2,0,1,4:T(8,128)} copy(f32[16,1,32,8,8,256]{5,4,3,2,1,0:T(8,128)} %param.9) | data formatting | bytes 67108864 | tf_op args[0]
  55.9 7.1 all-to-all-start
  64.4 5.8 all-reduce.1
  70.2 5.0 all_gather.11
  75.2 5.2 all_gather.14
  81.5 3.5 reshape.369
  85.0 30.9 %convolution_bitcast_fusion = f32[256,256,16,8]{1,2,3,0:T(8,128)} fusion(f32[4,2,256,256,1]{3,2,1,0,4:T(8,128)S(1)} %bitcast.118, f32[16,8,4,2]{0,1,3,2:T(8,128)S(1)} %convolution_bitcast_fusion.1), kind=kOutput, calls=%fused_computation.12 | convolution fusion | flops 805306368 | bytes 35655680 | tf_op jit(solution)/shard_map/absp,spxy->axby/dot_general | solution.py:101
  115.9 34.4 %copy.72 = f32[256,256,16,8]{0,1,3,2:T(8,128)} copy(f32[256,256,16,8]{1,2,3,0:T(8,128)} %convolution_bitcast_fusion) | data formatting | bytes 67108864 | tf_op jit(solution)/shard_map/absp,spxy->axby/dot_general | solution.py:101
  150.3 637.5 %all-to-all-done = f32[16,1,32,8,8,256]{5,3,2,0,1,4:T(8,128)} async-done(((f32[16,1,32,8,8,256]{5,3,2,0,1,4:T(8,128)}), f32[16,1,32,8,8,256]{5,3,2,0,1,4:T(8,128)}, u32[]{:S(2)}, u32[]{:S(2)}) %all-to-all-start) | async-done | bytes 33554464 | tf_op jit(solution)/shard_map/all_to_all | solution.py:36
  787.9 22.9 %copy.68 = f32[16,1,32,8,8,256]{5,3,2,4,0,1:T(8,128)} copy(f32[16,1,32,8,8,256]{5,3,2,0,1,4:T(8,128)} %all-to-all-done) | data formatting | bytes 67108864 | tf_op jit(solution)/shard_map/all_to_all | solution.py:36
  810.7 35.0 %copy.73 = f32[16,256,8,256]{1,3,2,0:T(8,128)} copy(f32[16,256,8,256]{3,2,1,0:T(8,128)} %bitcast.110) | data formatting | bytes 67108864 | tf_op jit(solution)/shard_map/reshape | solution.py:39
  845.7 33.5 %bitcast_add_fusion.1 = f32[16,256,8,256]{1,3,2,0:T(8,128)} fusion(f32[16,256,8,256]{1,3,2,0:T(8,128)} %copy.73, f32[256,256,16,8]{0,1,3,2:T(8,128)} %copy.72), kind=kLoop, calls=%fused_computation.7 | loop fusion | flops 8388608 | bytes 100663296 | tf_op jit(solution)/shard_map/add | solution.py:101
  879.2 32.0 %copy.74 = f32[16,256,8,256]{3,1,2,0:T(8,128)} copy(f32[16,256,8,256]{1,3,2,0:T(8,128)} %bitcast_add_fusion.1) | data formatting | bytes 67108864 | tf_op jit(solution)/shard_map/add | solution.py:101
  911.3 33.6 %fusion.1 = f32[16,256,8,256]{1,3,2,0:T(8,128)} fusion(f32[16,256,8,256]{1,3,2,0:T(8,128)} %bitcast_add_fusion.1, f32[16,256,8,256]{3,1,2,0:T(8,128)} %copy.74, pred[16,8]{1,0:T(8,128)(4,1)S(1)} %get-tuple-element.44), kind=kLoop, calls=%fused_computation.6 | loop fusion | flops 25165824 | bytes 100663424 | tf_op jit(solution)/shard_map/jit(_where)/select_n | solution.py:105
  947.0 11.7 cholesky.50
  958.8 9.8 custom-call.15
  969.1 11.7 cholesky.105
  983.7 4.5 slice.100
  988.3 5.8 copy.76
  994.1 5.7 copy.77
  999.7 14.5 all-reduce.5.cloned.1.call-done
  1015.3 3.8 while.2
  1019.1 19.7 %custom-call.16 = f32[2,128,128]{1,2,0:T(8,128)S(1)} custom-call(f32[2,128,128]{2,1,0:T(8,128)S(1)} %get-tuple-element.24), custom_call_target="InvertDiagBlocksLowerTriangular" | custom-call | tf_op jit(solution)/shard_map/jit(_solve_triangular)/triangular_solve | solution.py:112
  1038.8 3.6 fusion.4
  1042.4 1.9 convolution_subtract_fusion.1
  1044.4 1.9 fusion.18
  1046.3 2.4 maximum_bitcast_fusion
  1048.7 5.6 copy.94
  1054.3 4.7 select_select_fusion
  1059.1 156.5 %all-reduce.7.cloned.1.call-done = f32[16,256,256]{2,1,0:T(8,128)} async-done(((f32[16,256,256]{2,1,0:T(8,128)}), f32[16,256,256]{2,1,0:T(8,128)}) %all-reduce.7.cloned.1.call-update) | async-done | bytes 4194320 | tf_op jit(solution)/shard_map/psum | solution.py:15
  1215.6 1.7 collective-permute-start.2
  1217.3 89.6 %collective-permute-done = f32[16,256,256]{2,1,0:T(8,128)} collective-permute-done((f32[16,256,256]{2,1,0:T(8,128)}, f32[16,256,256]{2,1,0:T(8,128)}, u32[]{:S(2)}, u32[]{:S(2)}) %collective-permute-start) | collective-permute-done | bytes 4194336 | tf_op jit(solution)/shard_map/ppermute | solution.py:126
  1307.0 5.5 copy.83
  1312.7 42.4 %collective-permute-done.1 = f32[16,256,256]{2,1,0:T(8,128)} collective-permute-done((f32[16,256,256]{2,1,0:T(8,128)}, f32[16,256,256]{2,1,0:T(8,128)}, u32[]{:S(2)}, u32[]{:S(2)}) %collective-permute-start.1) | collective-permute-done | bytes 4194336 | tf_op jit(solution)/shard_map/ppermute | solution.py:126
  1355.2 6.5 pad_maximum_fusion
  1361.7 6.3 fusion.47
  1368.0 7.7 gather_fusion.1
  1375.6 7.7 gather_fusion
  1383.3 11.8 pad_maximum_fusion.1
  1395.1 34.9 %convolution_subtract_fusion = f32[16,256,8,256]{1,3,2,0:T(8,128)} fusion(f32[16,256,8,256]{1,3,2,0:T(8,128)} %fusion.1, f32[16,256,256]{2,1,0:T(8,128)S(1)} %copy-done.4, f32[4,8,2,256,256]{4,3,2,1,0:T(8,128)} %bitcast.113, s32[]{:T(128)S(6)} %select_n.164, s32[]{:T(128)S(6)} %select_n.167), kind=kOutput, calls=%fused_computation.11 | convolution fusion | flops 25778192384 | bytes 73400328 | tf_op jit(solution)/shard_map/asx,bqx->asbq/dot_general | solution.py:136
  1430.0 4.8 fusion.2
  1434.8 22.9 %select_bitcast_fusion = f32[16,1,256,8,1,256]{2,5,3,0,4,1:T(8,128)} fusion(f32[16,256,8,256]{1,3,2,0:T(8,128)} %fusion.2, pred[16,8]{1,0:T(8,128)(4,1)S(1)} %copy-done.7), kind=kLoop, calls=%fused_computation.8 | loop fusion | flops 8388608 | bytes 67108992 | tf_op jit(solution)/shard_map/reshape | solution.py:140
  1457.8 78.3 %copy.84 = f32[16,1,256,8,1,256]{5,4,3,2,1,0:T(1,128)} copy(f32[16,1,256,8,1,256]{2,5,3,0,4,1:T(8,128)} %select_bitcast_fusion) | data formatting | bytes 67108864 | tf_op jit(solution)/shard_map/reshape | solution.py:140
  (76 shorter events, 14.7 us)
Async XLA Ops:
  6.5 1.6 copy-start
  6.5 3.8 copy-start.8
  19.8 34.8 %all-to-all-start.1 = ((f32[4,2,65536]{2,1,0:T(2,128)}), f32[4,2,65536]{2,1,0:T(2,128)S(1)}, u32[]{:S(2)}, u32[]{:S(2)}) async-start(f32[4,2,65536]{2,1,0:T(2,128)} %fusion.33), calls=%async_computation.1 | async-start | bytes 4194304 | tf_op jit(solution)/shard_map/all_to_all | solution.py:75
  54.6 8.5 copy-start.11
  54.6 15.6 %copy-start.9 = (s32[1,1,8]{2,1,0:T(1,128)S(1)}, s32[1,1,8]{2,1,0:T(1,128)}, u32[]{:S(2)}) copy-start(s32[1,1,8]{2,1,0:T(1,128)} %param.11) | copy-start | bytes 100
  54.6 20.6 %copy-start.10 = (s32[1,1,8]{2,1,0:T(1,128)S(1)}, s32[1,1,8]{2,1,0:T(1,128)}, u32[]{:S(2)}) copy-start(s32[1,1,8]{2,1,0:T(1,128)} %param.12) | copy-start | bytes 100
  54.6 1.4 copy-start.5
  55.9 731.9 %all-to-all-start = ((f32[16,1,32,8,8,256]{5,3,2,0,1,4:T(8,128)}), f32[16,1,32,8,8,256]{5,3,2,0,1,4:T(8,128)}, u32[]{:S(2)}, u32[]{:S(2)}) async-start(f32[16,1,32,8,8,256]{5,3,2,0,1,4:T(8,128)} %copy.67), calls=%async_computation | async-start | bytes 67108864 | tf_op jit(solution)/shard_map/all_to_all | solution.py:36
  63.0 951.2 %all-reduce.5.cloned.1.call-start = ((), (), s32[]{:S(2)}) async-start(), calls=%async_computation.2 | async-start | bytes 524288 | tf_op jit(solution)/shard_map/psum | solution.py:15
  983.7 231.9 %all-reduce.7.cloned.1.call-start = ((), (), s32[]{:S(2)}) async-start(), calls=%async_computation.3 | async-start | bytes 8388608 | tf_op jit(solution)/shard_map/psum | solution.py:15
  1038.8 3.7 copy-start.3
  1215.6 91.4 %collective-permute-start = (f32[16,256,256]{2,1,0:T(8,128)}, f32[16,256,256]{2,1,0:T(8,128)}, u32[]{:S(2)}, u32[]{:S(2)}) collective-permute-start(f32[16,256,256]{2,1,0:T(8,128)} %all-reduce.7.cloned.1.call-done), channel_id=1, source_target_pairs={{0,8},{8,16},{16,24},{24,0},{1,9},{9,17},{17,25},{25,1},{2,10},{10... | collective-permute-start | bytes 12582920 | tf_op jit(solution)/shard_map/ppermute | solution.py:126
  1215.6 97.2 %collective-permute-start.2 = (f32[16,256,256]{2,1,0:T(8,128)}, f32[16,256,256]{2,1,0:T(8,128)}, u32[]{:S(2)}, u32[]{:S(2)}) collective-permute-start(f32[16,256,256]{2,1,0:T(8,128)} %all-reduce.7.cloned.1.call-done), channel_id=1, source_target_pairs={{8,0},{16,8},{24,16},{0,24},{9,1},{17,9},{25,17},{1,25},{10,2},{18... | collective-permute-start | bytes 12582920 | tf_op jit(solution)/shard_map/ppermute | solution.py:128
  1306.9 48.2 %collective-permute-start.1 = (f32[16,256,256]{2,1,0:T(8,128)}, f32[16,256,256]{2,1,0:T(8,128)}, u32[]{:S(2)}, u32[]{:S(2)}) collective-permute-start(f32[16,256,256]{2,1,0:T(8,128)} %collective-permute-done), channel_id=1, source_target_pairs={{0,8},{8,16},{16,24},{24,0},{1,9},{9,17},{17,25},{25,1},{2,10},{10... | collective-permute-start | bytes 12582920 | tf_op jit(solution)/shard_map/ppermute | solution.py:126
  1307.0 5.6 copy-start.6
  1383.3 11.8 copy-start.4
  1395.1 34.9 %copy-start.2 = (f32[16,256,1,256]{1,3,2,0:T(8,128)S(1)}, f32[16,256,1,256]{1,3,2,0:T(8,128)}, u32[]{:S(2)}) copy-start(f32[16,256,1,256]{1,3,2,0:T(8,128)} %copy.83) | copy-start | bytes 12582916
  1430.0 4.8 copy-start.7
  1457.8 78.3 %copy-start.1 = (f32[1,1,8,256,256]{4,3,2,1,0:T(8,128)S(1)}, f32[1,1,8,256,256]{4,3,2,1,0:T(8,128)}, u32[]{:S(2)}) copy-start(f32[1,1,8,256,256]{4,3,2,1,0:T(8,128)} %param.10) | copy-start | bytes 6291460
Sparse Core Ops, SparseCore 0:
  983.8 30.4 all-reduce.4
  1059.2 156.3 all-reduce.6
